TPU v7x, 512 devices: a whole 4x4x16 slice. The times are simulated.
512 devices in a mesh: grp: 16 (over z_lo, core), dev: 32 (over z_hi, x, y).
Axes of the slice: x: 4, y: 4, z: 16 (z_hi: 2, z_lo: 8; z = z_hi * 8 + z_lo), core: 2. Of those that a mesh axis runs over, the one named last changes fastest.
Arguments:
- records: bfloat16 [2048, 4, 2048], P(('grp', 'dev')), may hold values from -6 to 6
- usable: int32 [2048, 4], replicated, may hold values 0 or 1
- panel_ids: int32 [2], replicated, may hold values from 0 to 31
Outputs:
- xcorr: bfloat16 [2, 64, 2048, 512], P(None, None, ('grp', 'dev'))
Inputs may be any that keep to these rules, and one draw needn't show every extreme that they name: `panel_ids`: each entry names a panel.
All inputs are finite; a program needn't handle non-finite values.
Results may differ from a plain program's by a relative error of at most 0.0075.
Values may be sent and summed in bfloat16 or wider, within the bound.
A program may use at most 64 MiB of HBM per device.

v0:
```python
import math

import jax
import jax.numpy as jnp
from jax import lax
from jax.sharding import PartitionSpec as P

NLAG = 512
SRC_DEV = 2
STEPS = 2


def broadcast(block, axis, source):
    block = jnp.where(lax.axis_index(axis) == source, block, jnp.zeros_like(block))
    return lax.psum(block, axis)


def forward_table(length, bin_count):
    samples = jnp.arange(length, dtype=jnp.int32)[:, None]
    bin_index = jnp.arange(1, bin_count + 1, dtype=jnp.int32)[None, :]
    phases = 2.0 * math.pi / length * (samples * bin_index % length).astype(jnp.float32)
    return jnp.concatenate([jnp.cos(phases), -jnp.sin(phases)], axis=1).astype(jnp.bfloat16)


def lag_table(length, bin_count, lag_count):
    bin_index = jnp.arange(1, bin_count + 1, dtype=jnp.int32)[:, None]
    lag_index = jnp.arange(lag_count, dtype=jnp.int32)[None, :] - lag_count // 2
    phases = 2.0 * math.pi / length * (bin_index * lag_index % length).astype(jnp.float32)
    factor = 1.0 / math.sqrt(bin_count)
    return jnp.concatenate([jnp.cos(phases) * factor, -jnp.sin(phases) * factor], axis=0).astype(
        jnp.bfloat16
    )


def band_matrix(bin_count, radius):
    positions = jnp.arange(bin_count, dtype=jnp.int32)
    nearby = jnp.abs(positions[:, None] - positions[None, :]) <= radius
    return nearby.astype(jnp.float32) / (2 * radius + 1)


def whiten(records, bin_count, radius):
    row_count, windows, length = records.shape
    flattened = records.reshape(row_count * windows, length)
    spectra = jnp.dot(
        flattened, forward_table(length, bin_count), preferred_element_type=jnp.float32
    )
    real_part = spectra[:, :bin_count]
    imag_part = spectra[:, bin_count:]
    amplitude = jnp.sqrt(real_part * real_part + imag_part * imag_part)
    smooth = jnp.dot(amplitude, band_matrix(bin_count, radius), precision=lax.Precision.HIGHEST)
    whitened = spectra / (jnp.concatenate([smooth, smooth], axis=1) + 1e-06)
    return whitened.astype(jnp.bfloat16).reshape(row_count, windows, 2 * bin_count)


def paired(left, right):
    return jnp.einsum("swf,rwf->srf", left, right, preferred_element_type=jnp.float32)


def cross_spectra(sources, source_mask, receivers, receiver_mask, ltable, bin_count):
    source_re = sources[:, :, :bin_count]
    source_im = sources[:, :, bin_count:]
    recv_re = receivers[:, :, :bin_count]
    recv_im = receivers[:, :, bin_count:]
    real_sum = paired(source_re, recv_re) + paired(source_im, recv_im)
    imag_sum = paired(source_im, recv_re) - paired(source_re, recv_im)
    counts = jnp.dot(source_mask, receiver_mask.T, precision=lax.Precision.HIGHEST)
    denom = jnp.maximum(counts, 1.0)[:, :, None]
    stacked = jnp.concatenate([real_sum / denom, imag_sum / denom], axis=2).astype(jnp.bfloat16)
    source_count = sources.shape[0]
    recv_count = receivers.shape[0]
    lagged = jnp.dot(
        stacked.reshape(source_count * recv_count, 2 * bin_count),
        ltable,
        preferred_element_type=jnp.float32,
    )
    return lagged.reshape(source_count, recv_count, ltable.shape[1]).astype(jnp.bfloat16)


def on_device(records, usable, panel_ids):
    channels, windows, length = records.shape
    bin_count = length // 2
    radius = bin_count // 16
    halves = channels // SRC_DEV
    group_count = lax.axis_size("grp")
    member_count = lax.axis_size("dev")
    whitened = whiten(records, bin_count, radius)
    first_channel = (lax.axis_index("grp") * member_count + lax.axis_index("dev")) * channels
    own_mask = lax.dynamic_slice_in_dim(usable, first_channel, channels, 0)
    masked = whitened * own_mask.astype(jnp.bfloat16)[:, :, None]
    receiver_mask = own_mask.astype(jnp.float32)
    grouped_mask = usable.astype(jnp.float32).reshape(
        group_count, member_count, halves, SRC_DEV, windows
    )
    ltable = lag_table(length, bin_count, NLAG)
    results = []
    for step_index in range(STEPS):
        chosen = panel_ids[step_index]
        owning = chosen // halves
        within = chosen % halves
        source_rows = lax.dynamic_slice_in_dim(masked, within * SRC_DEV, SRC_DEV, 0)
        source_mask = grouped_mask[owning][:, within].reshape(member_count * SRC_DEV, windows)
        gathered = lax.all_gather(source_rows, "dev", axis=0, tiled=True)
        whole_panel = broadcast(gathered, "grp", owning)
        results.append(
            cross_spectra(whole_panel, source_mask, masked, receiver_mask, ltable, bin_count)
        )
    return jnp.stack(results)


def solution(mesh):
    placed = (P(("grp", "dev"), None, None), P(), P())
    return jax.shard_map(
        on_device,
        mesh=mesh,
        in_specs=placed,
        out_specs=P(None, None, ("grp", "dev"), None),
        check_vma=False,
    )
```

profile of v0, /device:TPU:1, one launch (start us, length us, event | category | flops | bytes accessed | tf_op | source)
XLA Modules:
  0.0 561.4 jit_solution(5559478100995310142)
XLA Ops:
  12.3 35.0 %cosine_convert_fusion = (bf16[2048,1024]{1,0:T(8,128)(2,1)}, bf16[2048,1024]{1,0:T(8,128)(2,1)}) fusion(s32[1024]{0:T(1024)S(1)} %iota_add_fusion), kind=kLoop, calls=%fused_computation.11 | loop fusion | flops 35651584 | bytes 8392704 | tf_op jit(solution)/shard_map/convert.6
  47.4 4.1 fusion.12
  52.7 2.6 copy.10
  55.2 1.7 broadcast_multiply_fusion
  57.0 3.0 constant_dynamic-slice_fusion.3
  60.0 3.5 copy.11
  63.6 1.8 copy.15
  66.6 112.6 %all-gather.3.cloned.1.call-done = bf16[64,4,2048]{2,1,0:T(4,128)(2,1)} async-done(((bf16[2,4,2048]{2,1,0:T(4,128)(2,1)}), bf16[64,4,2048]{2,1,0:T(4,128)(2,1)}) %all-gather.3.cloned.1.call-update) | async-done | bytes 1048592 | tf_op jit(solution)/shard_map/all_gather | solution.py:102
  179.3 4.4 copy.12
  183.6 1.9 broadcast_select_fusion.1
  185.6 98.8 %all-gather.5.cloned.1.call-done = bf16[64,4,2048]{2,1,0:T(4,128)(2,1)} async-done(((bf16[2,4,2048]{2,1,0:T(4,128)(2,1)}), bf16[64,4,2048]{2,1,0:T(4,128)(2,1)}) %all-gather.5.cloned.1.call-update) | async-done | bytes 1048592 | tf_op jit(solution)/shard_map/all_gather | solution.py:102
  284.4 4.3 copy.16
  288.7 1.9 broadcast_select_fusion
  293.5 10.0 %multiply_convert_fusion.1 = (bf16[1024,512]{1,0:T(8,128)(2,1)}, bf16[1024,512]{1,0:T(8,128)(2,1)}) fusion(s32[512]{0:T(512)S(1)} %iota_add_fusion.1, s32[1024]{0:T(1024)S(1)} %iota_add_fusion), kind=kLoop, calls=%fused_computation.39 | loop fusion | flops 9961472 | bytes 2103296 | tf_op jit(solution)/shard_map/convert.2
  303.6 192.7 %all-reduce.3.cloned.1.call-done = (bf16[64,4,2048]{0,1,2:T(4,128)(2,1)}, bf16[64,4,2048]{0,1,2:T(4,128)(2,1)}) async-done(((bf16[64,4,2048]{0,1,2:T(4,128)(2,1)}, bf16[64,4,2048]{0,1,2:T(4,128)(2,1)}), (bf16[64,4,2048]{0,1,2:T(4,128)(2,1)}, bf16[64,4,2048]{0,1,2:T(4,128)(2,1)})) %all-reduce.3.cloned.1.call-update) | async-done | bytes 2097168 | tf_op jit(solution)/shard_map/psum | solution.py:15
  496.3 1.7 fusion.105
  498.2 1.3 fusion.91
  499.5 1.3 fusion.103
  500.8 1.4 fusion.93
  502.2 1.3 fusion.101
  503.5 1.4 fusion.95
  504.9 1.3 fusion.99
  506.2 1.3 fusion.97
  507.6 2.6 fusion.51
  510.2 2.6 fusion.47
  512.8 2.6 fusion.45
  515.4 2.6 fusion.41
  518.0 2.2 fusion.25
  520.2 1.3 fusion.26
  521.5 13.7 %pad_maximum_fusion = bf16[64,4,2048]{0,1,2:T(4,128)(2,1)} fusion(bf16[64,4,1024]{0,1,2:T(4,128)(2,1)S(1)} %fusion.26, bf16[64,4,1024]{0,1,2:T(4,128)(2,1)S(1)} %copy-done.13), kind=kLoop, calls=%fused_computation.27 | loop fusion | flops 524288 | bytes 2097152 | tf_op jit(solution)/shard_map/concatenate | solution.py:68
  535.2 2.3 fusion.27
  538.9 12.7 %pad_maximum_fusion.1 = bf16[64,4,2048]{0,1,2:T(4,128)(2,1)S(1)} fusion(bf16[64,4,1024]{0,1,2:T(4,128)(2,1)S(1)} %fusion.28, bf16[64,4,1024]{0,1,2:T(4,128)(2,1)S(1)} %copy-done.12), kind=kLoop, calls=%fused_computation.29 | loop fusion | flops 524288 | bytes 2097152 | tf_op jit(solution)/shard_map/concatenate | solution.py:68
  (70 shorter events, 10.6 us)
Async XLA Ops:
  6.5 172.7 %all-gather.3.cloned.1.call-start = ((), (), s32[]{:S(2)}) async-start(), calls=%async_computation | async-start | bytes 1081344 | tf_op jit(solution)/shard_map/all_gather | solution.py:102
  12.3 35.0 %copy-start.14 = (bf16[4,4,2048]{2,1,0:T(4,128)(2,1)S(1)}, bf16[4,4,2048]{2,1,0:T(4,128)(2,1)}, u32[]{:S(2)}) copy-start(bf16[4,4,2048]{2,1,0:T(4,128)(2,1)} %param.3) | copy-start | bytes 196612
  63.5 220.8 %all-gather.5.cloned.1.call-start = ((), (), s32[]{:S(2)}) async-start(), calls=%async_computation.1 | async-start | bytes 1081344 | tf_op jit(solution)/shard_map/all_gather | solution.py:102
  65.4 430.9 %all-reduce.3.cloned.1.call-start = ((), (), s32[]{:S(2)}) async-start(), calls=%async_computation.2 | async-start | bytes 8388608 | tf_op jit(solution)/shard_map/psum | solution.py:15
  290.6 0.8 copy-start.15
  496.2 1.9 copy-start.1
  499.5 2.7 copy-start
  507.6 2.6 copy-start.9
  510.2 2.6 copy-start.10
  512.8 2.6 copy-start.11
  515.4 2.6 copy-start.8
  515.4 2.6 copy-start.17
  515.4 2.6 copy-start.21
  518.0 2.2 copy-start.7
  518.0 2.2 copy-start.20
  520.2 1.3 copy-start.13
  521.5 13.7 %copy-start.6 = (bf16[64,4,1024]{0,1,2:T(4,128)(2,1)S(1)}, bf16[64,4,1024]{0,1,2:T(4,128)(2,1)}, u32[]{:S(2)}) copy-start(bf16[64,4,1024]{0,1,2:T(4,128)(2,1)} %fusion.95) | copy-start | bytes 1572868
  521.5 13.7 %copy-start.16 = (f32[64,4]{0,1:T(4,128)S(1)}, f32[64,4]{0,1:T(4,128)}, u32[]{:S(2)}) copy-start(f32[64,4]{0,1:T(4,128)} %convolution_maximum_fusion) | copy-start | bytes 3076
  521.5 13.7 %copy-start.19 = (f32[1024,4,64]{2,1,0:T(4,128)S(1)}, f32[1024,4,64]{2,1,0:T(4,128)}, u32[]{:S(2)}) copy-start(f32[1024,4,64]{2,1,0:T(4,128)} %fusion.45) | copy-start | bytes 3145732
  535.2 2.3 copy-start.5
  535.2 2.3 copy-start.18
  537.5 1.3 copy-start.12
  538.9 12.8 %copy-start.2 = (bf16[64,4,2048]{0,1,2:T(4,128)(2,1)S(1)}, bf16[64,4,2048]{0,1,2:T(4,128)(2,1)}, u32[]{:S(2)}) copy-start(bf16[64,4,2048]{0,1,2:T(4,128)(2,1)} %pad_maximum_fusion) | copy-start | bytes 3145732
  538.9 12.8 %copy-start.3 = (bf16[1024,512]{1,0:T(8,128)(2,1)S(1)}, bf16[1024,512]{1,0:T(8,128)(2,1)}, u32[]{:S(2)}) copy-start(bf16[1024,512]{1,0:T(8,128)(2,1)} %get-tuple-element.11) | copy-start | bytes 3145732
  538.9 12.8 %copy-start.4 = (bf16[1024,512]{1,0:T(8,128)(2,1)S(1)}, bf16[1024,512]{1,0:T(8,128)(2,1)}, u32[]{:S(2)}) copy-start(bf16[1024,512]{1,0:T(8,128)(2,1)} %get-tuple-element.12) | copy-start | bytes 3145732
Sparse Core Ops, SparseCore 0:
  63.7 115.5 all-gather.2
  183.5 100.7 all-gather.4
  290.7 205.4 all-reduce.2
where the time goes:
time: 570 us; the launch traced here: 561 us
  waiting for transfers between devices  404 us (71%)
  other arithmetic  77.8 us (14%)
  local copies, waits for them, and re-layouts  34.7 us (6%)
  matrix products  26 us (5%)
  between operations  18.6 us (3%)
    all_gather x2, waiting for transfers between devices, on_device(): gathered = lax.all_gather(source_rows, 'dev', axis=0, tiled=True)  211 us
    psum x1, waiting for transfers between devices, broadcast(): return lax.psum(block, axis)  193 us
    another operation x2, other arithmetic  45.1 us
    concatenate x2, other arithmetic, cross_spectra(): jnp.concatenate([real_sum / denom, imag_sum / denom], axis=2)  26.4 us
    dot_general x8, matrix products, paired(): jnp.einsum('swf,rwf->srf', left, right, preferred_element_type=jnp.float32)  17.5 us
  transfers between devices with their start and end apart: 3, of which 3 were waited for; matrix products, arithmetic and copies ran while one was open for 4% of the time, Pallas kernels for 0%

commit v1 on v0

v1 whole, which is shorter than its diff:
```python
import math

import jax
import jax.numpy as jnp
import ml_dtypes
import numpy as np
from jax import lax
from jax.experimental import pallas as pl
from jax.experimental.pallas import tpu as pltpu
from jax.sharding import PartitionSpec as P

L = 2048
NF = 1024
RADIUS = 64
NLAG = 512
F32 = jnp.float32
BF16 = jnp.bfloat16
MESH = pl.DeviceIdType.MESH


def bins_of():
    lane = np.arange(128)
    bins = np.zeros((8, 128), np.int64)
    bins[0] = np.where(lane < 64, 16 * lane + 8, 16 * (lane - 63))
    for r in range(1, 8):
        bins[r] = 16 * lane + r
    return bins


def split_table(table):
    high = table.astype(ml_dtypes.bfloat16)
    low = (table - high.astype(np.float64)).astype(ml_dtypes.bfloat16)
    return high, low


def make_tables():
    bins = bins_of()
    natural = np.where(bins > NF, L - bins, bins)
    b = np.arange(128)
    angle = 2 * np.pi * np.outer(b, b) / 128
    cos, sin = np.cos(angle), np.sin(angle)
    dft = np.block([[cos, -sin], [sin, cos]])
    special = np.zeros((384, 256))
    for lane in range(64):
        special[128:256, lane] = cos[:, lane]
        special[256:384, lane] = sin[:, lane]
        special[128:256, 128 + lane] = -sin[:, lane]
        special[256:384, 128 + lane] = cos[:, lane]
    for lane in range(64, 128):
        special[0:128, lane] = np.cos(2 * np.pi * b * (lane - 63) / 128)
        special[0:128, 128 + lane] = -np.sin(2 * np.pi * b * (lane - 63) / 128)
    r = np.arange(16)[:, None]
    twiddle = 2 * np.pi * r * b[None, :] / L
    turn = np.stack([np.cos(twiddle), np.sin(twiddle)]).astype(np.float32)

    def near(left, right):
        return (np.abs(natural[left][:, None] - natural[right][None, :]) <= RADIUS).astype(np.float64)

    band = np.concatenate([near(1, 2), near(2, 2), near(3, 2), near(0, 2)], axis=0)
    band0 = np.concatenate([near(1, 0), near(0, 0)], axis=0)
    lag = np.arange(NLAG) - NLAG // 2
    phase = 2 * np.pi * ((bins.reshape(-1)[:, None] * lag[None, :]) % L) / L
    ltable = np.concatenate([np.cos(phase), -np.sin(phase)], axis=0) / math.sqrt(NF)
    bf = ml_dtypes.bfloat16
    bands = np.concatenate([np.concatenate([band[:256], band[256:]], axis=1), np.concatenate([band0[:128], band0[128:]], axis=1)], axis=0)
    packed = np.concatenate([*split_table(dft), *split_table(special), bands.astype(bf)], axis=0)
    return packed, turn, ltable.astype(bf)


def split(values):
    high = values.astype(BF16)
    return high, (values - high.astype(F32)).astype(BF16)


def dot(left, right):
    return jnp.dot(left, right, preferred_element_type=F32)


def transform(rows, tab_ref, turn_ref):
    count = rows.shape[0]
    x = [rows[:, 128 * a : 128 * a + 128] for a in range(16)]
    even = [None] + [x[a] + x[16 - a] for a in range(1, 8)]
    odd = [None] + [x[a] - x[16 - a] for a in range(1, 8)]
    parts_re, parts_im = [], []
    for r in range(9):
        re = x[0] + x[8] if r % 2 == 0 else x[0] - x[8]
        im = None
        for a in range(1, 8):
            c = math.cos(2 * math.pi * ((a * r) % 16) / 16)
            s = math.sin(2 * math.pi * ((a * r) % 16) / 16)
            if abs(c) > 1e-9:
                re = re + even[a] * c
            if abs(s) > 1e-9:
                im = odd[a] * -s if im is None else im + odd[a] * -s
        parts_re.append(re)
        parts_im.append(im)
    turned = []
    for r in range(1, 8):
        c, s = turn_ref[0, r : r + 1, :], turn_ref[1, r : r + 1, :]
        turned.append(jnp.concatenate([parts_re[r] * c + parts_im[r] * s, parts_im[r] * c - parts_re[r] * s], axis=1))
    y = jnp.concatenate(turned, axis=0)
    c, s = turn_ref[0, 8:9, :], turn_ref[1, 8:9, :]
    y0 = jnp.concatenate([parts_re[0], parts_re[8] * c, -(parts_re[8] * s)], axis=1)

    def product(values, at):
        high, low = split(values)
        n, depth = values.shape
        both = dot(jnp.concatenate([high, low], axis=0), tab_ref[at : at + depth])
        return both[:n] + both[n:] + dot(high, tab_ref[at + depth : at + 2 * depth])

    spectra = product(y, 0)
    spectra0 = product(y0, 512)
    re = [spectra0[:, :128]] + [spectra[count * j : count * j + count, :128] for j in range(7)]
    im = [spectra0[:, 128:]] + [spectra[count * j : count * j + count, 128:] for j in range(7)]
    return re, im


def running_mean(amplitude, tab_ref):
    count = amplitude[0].shape[0]
    below = [None, jnp.zeros_like(amplitude[0])]
    for r in range(2, 9):
        below.append(below[r - 1] + amplitude[r - 1])
    total = below[8]
    left = jnp.concatenate(
        [
            jnp.concatenate([below[r], amplitude[r], total - below[r] - amplitude[r], amplitude[0]], axis=1)
            for r in range(1, 8)
        ],
        axis=0,
    )
    left0 = jnp.concatenate([total, amplitude[0]], axis=1)

    def product(values, at):
        high, low = split(values)
        half = values.shape[1] // 2
        both = jnp.concatenate([high, low], axis=0)
        both = dot(both[:, :half], tab_ref[at : at + half, :128]) + dot(both[:, half:], tab_ref[at : at + half, 128:])
        return both[: values.shape[0]] + both[values.shape[0] :]

    sums = product(left, 1280)
    sums0 = product(left0, 1536)
    scale = 1.0 / (2 * RADIUS + 1)
    return [sums0 * scale] + [sums[count * j : count * j + count] * scale for j in range(7)]


def kernel(
    panel_ids_ref,
    x_hbm,
    usable_hbm,
    tab_hbm,
    turn_hbm,
    lt_hbm,
    out_ref,
    x_ref,
    usable_ref,
    tab_ref,
    turn_ref,
    units,
    picks,
    panel,
    own,
    other,
    recv,
    lhs,
    lt_ref,
    scales,
    outbox,
    in_sem,
    unit_send,
    unit_recv,
    other_send,
    other_recv,
    line_send,
    line_recv,
    plane_send,
    plane_recv,
    out_send,
    out_recv,
):
    g = lax.axis_index("grp")
    d = lax.axis_index("dev")
    z_lo, c = g // 2, g % 2
    z_hi, xx, yy = d // 16, (d // 4) % 4, d % 4
    mate = z_lo * 2 + (1 - c)

    loads = [
        pltpu.make_async_copy(source, target, in_sem.at[n])
        for n, (source, target) in enumerate(
            [(x_hbm, x_ref), (turn_hbm, turn_ref), (tab_hbm, tab_ref), (usable_hbm, usable_ref), (lt_hbm, lt_ref)]
        )
    ]
    for load in loads:
        load.start()

    barrier = pltpu.get_barrier_semaphore()

    def hello(grp, dev):
        pl.semaphore_signal(barrier, inc=1, device_id=(grp, dev), device_id_type=MESH)

    def hello_grp(k, carry):
        hello((g + k) % 16, d)
        return carry

    lax.fori_loop(1, 16, hello_grp, 0)

    def hello_line(k, carry):
        hello(2 * k + c, (1 - z_hi) * 16 + d % 16)
        return carry

    lax.fori_loop(0, 8, hello_line, 0)

    def hello_plane(k, carry):
        hello(g, z_hi * 16 + ((xx + k) % 4) * 4 + yy)
        hello(g, z_hi * 16 + xx * 4 + (yy + k) % 4)
        return carry

    lax.fori_loop(1, 4, hello_plane, 0)

    for load in loads[:4]:
        load.wait()
    rows = jnp.concatenate([x_ref[ch].astype(F32) for ch in range(4)], axis=0)
    spec_re, spec_im = transform(rows, tab_ref, turn_ref)
    amplitude = [jnp.sqrt(re * re + im * im) for re, im in zip(spec_re, spec_im)]
    smooth = running_mean(amplitude, tab_ref)

    lane16 = lax.broadcasted_iota(jnp.int32, (16, 128), 1)
    row16 = lax.broadcasted_iota(jnp.int32, (16, 128), 0)

    def mask_of(group):
        block = usable_ref[:, pl.ds(pl.multiple_of(group * 128, 128), 128)].astype(F32)
        tiled = jnp.concatenate([block] * 4, axis=0)
        chosen = jnp.where(lane16 == 4 * d + row16 // 4, tiled, 0.0)
        return jnp.sum(chosen, axis=1, keepdims=True)

    own_mask = mask_of(g)
    mate_mask = mask_of(mate)

    upper = [(jnp.full((8, 128), panel_ids_ref[t]) & 1) == 1 for t in range(2)]
    for k in range(8):
        inverse = 1.0 / (smooth[k] + 1e-06)
        re = (spec_re[k] * inverse).astype(BF16).astype(F32) * own_mask
        im = (spec_im[k] * inverse).astype(BF16).astype(F32) * own_mask
        own[k] = re.astype(BF16)
        own[8 + k] = im.astype(BF16)
        for t in range(2):
            pair = jnp.concatenate(
                [jnp.where(upper[t], re[8:], re[:8]), jnp.where(upper[t], im[8:], im[:8])], axis=0
            )
            units[2 * k + t] = pair.astype(BF16)

    pl.semaphore_wait(barrier, 29)

    def send_unit(k, carry):
        to = (g + k) % 16
        pltpu.make_async_remote_copy(
            src_ref=units.at[to],
            dst_ref=picks.at[g],
            send_sem=unit_send,
            recv_sem=unit_recv,
            device_id=(to, d),
            device_id_type=MESH,
        ).start()
        return carry

    lax.fori_loop(1, 16, send_unit, 0)
    to_mate = pltpu.make_async_remote_copy(
        src_ref=own,
        dst_ref=other,
        send_sem=other_send,
        recv_sem=other_recv,
        device_id=(mate, d),
        device_id_type=MESH,
    )
    to_mate.start()
    picks[g] = units[g]

    pltpu.make_async_copy(picks.at[pl.ds(0, 15)], picks.at[pl.ds(0, 15)], unit_recv).wait()
    chosen = panel_ids_ref[c]
    owner = jnp.full((16, 128), chosen) >> 1
    pick = jnp.where(owner == 0, picks[0].astype(F32), 0.0)
    for k in range(1, 16):
        pick = jnp.where(owner == k, picks[k].astype(F32), pick)
    panel[xx, yy, z_hi, z_lo] = pick.astype(BF16)

    mine = panel.at[xx, yy, z_hi, z_lo]

    def send_line(k, carry):
        z = (z_hi * 8 + z_lo + k) % 16
        pltpu.make_async_remote_copy(
            src_ref=mine,
            dst_ref=mine,
            send_sem=line_send,
            recv_sem=line_recv,
            device_id=((z % 8) * 2 + c, (z // 8) * 16 + d % 16),
            device_id_type=MESH,
        ).start()
        return carry

    lax.fori_loop(1, 16, send_line, 0)

    low = lax.broadcasted_iota(jnp.int32, (8, 128), 0) < 4

    def spread(side, source):
        def one(p, carry):
            tile = source[p].astype(F32)
            for pair in range(2):
                rows8 = tile[8 * pair : 8 * pair + 8]
                turned = pltpu.roll(rows8, 4, 0)
                recv[side, p, 2 * pair] = jnp.where(low, rows8, turned)
                recv[side, p, 2 * pair + 1] = jnp.where(low, turned, rows8)
            return carry

        lax.fori_loop(0, 16, one, 0)

    spread(0, own)
    to_mate.wait_recv()
    spread(1, other)

    block = usable_ref[:, :128]
    for k in range(1, 16):
        block = jnp.where(owner[:4] == k, usable_ref[:, 128 * k : 128 * k + 128], block)
    block = block.astype(F32)
    weights = jnp.concatenate([block] * 8, axis=0) * jnp.concatenate([own_mask, mate_mask], axis=0)
    row = lax.broadcasted_iota(jnp.int32, (512, 128), 0)
    lane = lax.broadcasted_iota(jnp.int32, (512, 128), 1)
    at_x = (xx + row // 128) % 4
    at_y = (yy + (row // 32) % 4) % 4
    at_dev = ((row // 16) % 2) * 16 + at_x * 4 + at_y
    half = jnp.full((512, 128), chosen) & 1
    picked = jnp.where(lane == at_dev * 4 + half * 2 + (row // 4) % 2, 1.0, 0.0).astype(BF16)
    counts = lax.dot_general(picked, weights.astype(BF16), (((1,), (1,)), ((), ())), preferred_element_type=F32)
    row32 = lax.broadcasted_iota(jnp.int32, (512, 32), 0)
    lane32 = lax.broadcasted_iota(jnp.int32, (512, 32), 1)
    match = lane32 // 4 == ((row32 // 8) % 2) * 4 + row32 % 4
    count = jnp.sum(jnp.where(match, counts, 0.0), axis=1, keepdims=True)
    scales[...] = jnp.broadcast_to(1.0 / jnp.maximum(count, 1.0), (512, 128))

    pltpu.make_async_copy(picks.at[pl.ds(0, 15)], picks.at[pl.ds(0, 15)], line_recv).wait()

    def send_block(h, bx, by, tx, ty):
        pltpu.make_async_remote_copy(
            src_ref=panel.at[bx, by, h],
            dst_ref=panel.at[bx, by, h],
            send_sem=plane_send,
            recv_sem=plane_recv.at[h, bx, by],
            device_id=(g, z_hi * 16 + tx * 4 + ty),
            device_id_type=MESH,
        ).start()

    def wait_block(h, bx, by):
        ref = panel.at[bx, by, h]
        pltpu.make_async_copy(ref, ref, plane_recv.at[h, bx, by]).wait()

    def send_first(k, carry):
        send_block(0, xx, yy, (xx + k) % 4, yy)
        send_block(1, xx, yy, xx, (yy + k) % 4)
        return carry

    def send_own(k, carry):
        send_block(0, xx, yy, xx, (yy + k) % 4)
        send_block(1, xx, yy, (xx + k) % 4, yy)
        return carry

    lax.fori_loop(1, 4, send_first, 0)
    lax.fori_loop(1, 4, send_own, 0)

    def forward(k, carry):
        bx, by = (xx + k) % 4, (yy + k) % 4
        wait_block(0, bx, yy)

        def on_y(m, inner):
            send_block(0, bx, yy, xx, (yy + m) % 4)
            return inner

        lax.fori_loop(1, 4, on_y, 0)
        wait_block(1, xx, by)

        def on_x(m, inner):
            send_block(1, xx, by, (xx + m) % 4, yy)
            return inner

        lax.fori_loop(1, 4, on_x, 0)
        return carry

    lax.fori_loop(1, 4, forward, 0)

    wait_block(1, (xx + 1) % 4, yy)
    wait_block(1, (xx + 2) % 4, yy)
    wait_block(1, (xx + 3) % 4, yy)
    wait_block(0, xx, (yy + 1) % 4)
    wait_block(0, xx, (yy + 2) % 4)
    wait_block(0, xx, (yy + 3) % 4)
    loads[4].wait()

    sub = lax.broadcasted_iota(jnp.int32, (8, 128), 0)
    even1 = sub % 2 == 0
    even2 = (sub // 2) % 2 == 0

    def fold(v):
        first = jnp.where(even1, v[0] + pltpu.roll(v[0], 7, 0), v[1] + pltpu.roll(v[1], 1, 0))
        second = jnp.where(even1, v[2] + pltpu.roll(v[2], 7, 0), v[3] + pltpu.roll(v[3], 1, 0))
        return jnp.where(even2, first + pltpu.roll(first, 6, 0), second + pltpu.roll(second, 2, 0))

    def cross(line, bx, by, h):
        slot = line * 2 + h
        for k in range(8):
            both = panel[bx, by, h, k].astype(F32)
            a, b = both[:8], both[8:]
            re_rows, im_rows = [], []
            for side in range(2):
                re, im = [], []
                for r in range(4):
                    cc, ee = recv[side, k, r], recv[side, 8 + k, r]
                    re.append(a * cc + b * ee)
                    im.append(b * cc - a * ee)
                re_rows.append(fold(re))
                im_rows.append(fold(im))
            at = pl.ds(pl.multiple_of(slot * 16, 16), 16)
            lhs[at, 128 * k : 128 * k + 128] = jnp.concatenate(re_rows, axis=0).astype(BF16)
            lhs[at, 1024 + 128 * k : 1152 + 128 * k] = jnp.concatenate(im_rows, axis=0).astype(BF16)

    def quarter(q, carry):
        bx = (xx + q) % 4

        def one_line(m, inner):
            by = (yy + m) % 4
            cross(q * 4 + m, bx, by, 0)
            cross(q * 4 + m, bx, by, 1)
            return inner

        lax.fori_loop(0, 4, one_line, 0)
        at = pl.ds(pl.multiple_of(q * 128, 128), 128)
        lagged = dot(lhs[at, :], lt_ref[...]) * jnp.concatenate([scales[at, :]] * 4, axis=1)
        for m in range(4):
            by = (yy + m) % 4
            for h in range(2):
                base = m * 32 + h * 16
                s = (h * 16 + bx * 4 + by) * 2
                for i in range(2):
                    out_ref[c, s + i] = lagged[base + 4 * i : base + 4 * i + 4].astype(BF16)
                    outbox[s + i] = lagged[base + 8 + 4 * i : base + 12 + 4 * i].astype(BF16)
        return carry

    quarter(0, 0)

    def later(q, carry):
        bx = (xx + q) % 4

        def wait_line(m, inner):
            by = (yy + m) % 4
            wait_block(0, bx, by)
            wait_block(1, bx, by)
            return inner

        lax.fori_loop(1, 4, wait_line, 0)
        return quarter(q, carry)

    lax.fori_loop(1, 4, later, 0)

    to_out = pltpu.make_async_remote_copy(
        src_ref=outbox,
        dst_ref=out_ref.at[c],
        send_sem=out_send,
        recv_sem=out_recv,
        device_id=(mate, d),
        device_id_type=MESH,
    )
    to_out.start()

    pltpu.make_async_copy(picks.at[pl.ds(0, 15)], picks.at[pl.ds(0, 15)], unit_send).wait()
    pltpu.make_async_copy(picks.at[pl.ds(0, 15)], picks.at[pl.ds(0, 15)], line_send).wait()
    to_mate.wait_send()
    for part in range(3):
        ref = panel.at[part]
        pltpu.make_async_copy(ref, ref, plane_send).wait()
    ref = panel.at[3, pl.ds(0, 3)]
    pltpu.make_async_copy(ref, ref, plane_send).wait()
    to_out.wait_send()
    pltpu.make_async_copy(outbox, outbox, out_recv).wait()


def on_device(records, usable, panel_ids):
    tables = [jnp.asarray(t) for t in make_tables()]
    vmem = pl.BlockSpec(memory_space=pltpu.VMEM)
    dma = pltpu.SemaphoreType.DMA
    return pl.pallas_call(
        kernel,
        out_shape=jax.ShapeDtypeStruct((2, 64, 4, NLAG), BF16),
        in_specs=[pl.BlockSpec(memory_space=pltpu.SMEM)] + [pl.BlockSpec(memory_space=pltpu.HBM)] * 5,
        out_specs=vmem,
        scratch_shapes=[
            pltpu.VMEM((4, 4, 2048), BF16),
            pltpu.VMEM((4, 2048), jnp.int32),
            pltpu.VMEM((1664, 256), BF16),
            pltpu.VMEM((2, 16, 128), F32),
            pltpu.VMEM((16, 16, 128), BF16),
            pltpu.VMEM((16, 16, 128), BF16),
            pltpu.VMEM((4, 4, 2, 8, 16, 128), BF16),
            pltpu.VMEM((16, 16, 128), BF16),
            pltpu.VMEM((16, 16, 128), BF16),
            pltpu.VMEM((2, 16, 4, 8, 128), F32),
            pltpu.VMEM((512, 2048), BF16),
            pltpu.VMEM((2048, NLAG), BF16),
            pltpu.VMEM((512, 128), F32),
            pltpu.VMEM((64, 4, NLAG), BF16),
            dma((5,)),
            dma,
            dma,
            dma,
            dma,
            dma,
            dma,
            dma,
            dma((2, 4, 4)),
            dma,
            dma,
        ],
        compiler_params=pltpu.CompilerParams(
            collective_id=0, has_side_effects=True, vmem_limit_bytes=60 * 1024 * 1024
        ),
    )(panel_ids, records, usable.T, *tables)


def solution(mesh):
    return jax.shard_map(
        on_device,
        mesh=mesh,
        in_specs=(P(("grp", "dev"), None, None), P(), P()),
        out_specs=P(None, None, ("grp", "dev"), None),
        check_vma=False,
    )
```

time: 570 us -> 49 us (0.09); the launches traced: 561 us -> 48.8 us
  waiting for transfers between devices: 404 us -> 0 us
  other arithmetic: 77.8 us -> 0 us
  Pallas kernels: 0 us -> 46.8 us
  local copies, waits for them, and re-layouts: 34.7 us -> 2.02 us
  matrix products: 26 us -> 0 us
  between operations: 18.6 us -> 0.01 us
    all_gather x2 -> x0, waiting for transfers between devices: 211 us -> none  [on_device(): gathered = lax.all_gather(source_rows, 'dev', axis=0, tiled=True)]
    psum x1 -> x0, waiting for transfers between devices: 193 us -> none  [broadcast(): return lax.psum(block, axis)]
    pallas_call x0 -> x1, Pallas kernels: none -> 46.8 us  [on_device(): pl.pallas_call(kernel, out_shape=jax.ShapeDtypeStruct((2, 64, 4, NLAG), B...]
    another operation x3 -> x0, other arithmetic: 45.1 us -> none
    concatenate x2 -> x0, other arithmetic: 26.4 us -> none  [cross_spectra(): jnp.concatenate([real_sum / denom, imag_sum / denom], axis=2)]
    dot_general x14 -> x0, matrix products: 26 us -> none  [the longest x8 17.5 us: paired(): jnp.einsum('swf,rwf->srf', left, right, preferred_element_type=jnp.float32)]
    dot_general x8 -> x0, local copies, waits for them, and re-layouts: 11.1 us -> none  [paired(): jnp.einsum('swf,rwf->srf', left, right, preferred_element_type=jnp.float32)]
    all_gather x2 -> x0, local copies, waits for them, and re-layouts: 8.72 us -> none  [on_device(): gathered = lax.all_gather(source_rows, 'dev', axis=0, tiled=True)]
  transfers between devices with their start and end apart: 3 -> 0, of which waited for: 3 -> 0; matrix products, arithmetic and copies ran while one was open for 4% -> 0% of each run, Pallas kernels for 0% -> 0%
where the time goes in v1:
time: 49 us; the launch traced here: 48.8 us
  Pallas kernels  46.8 us (96%)
  local copies, waits for them, and re-layouts  2.02 us (4%)
    pallas_call x1, Pallas kernels, on_device(): pl.pallas_call(kernel, out_shape=jax.ShapeDtypeStruct((2, 64, 4, NLAG), B...  46.8 us
    unnamed x1, local copies, waits for them, and re-layouts  2.02 us

profile of v1, /device:TPU:1, one launch (start us, length us, event | category | flops | bytes accessed | tf_op | source)
XLA Modules:
  0.0 48.8 jit_solution(7945764473187292540)
XLA Ops:
  0.0 46.8 %shard_map.64 = bf16[2,64,4,512]{3,2,1,0:T(4,128)(2,1)} custom-call(s32[2]{0:T(128)} %panel_ids_ref.1, bf16[4,4,2048]{2,1,0:T(4,128)(2,1)} %x_hbm.1, s32[4,2048]{1,0:T(4,128)} %bitcast.1, bf16[1664,256]{1,0:T(8,128)(2,1)} %constant.6.clone.tab_hbm, f32[2,16,128]{2,1,0:T(8,128)} %constant.7.clone.turn_hbm, bf16[2048,512]{1,0:T(8,128)(2,1)} %constant.8.clone.lt_hbm), custom_call_target="tpu_custom_call" | custom-call | tf_op jit(solution)/shard_map/pallas_call | solution.py:486
  46.8 2.0 %copy.8 = bf16[2,64,4,512]{3,2,1,0:T(4,128)(2,1)} copy(bf16[2,64,4,512]{3,2,1,0:T(4,128)(2,1)} %shard_map.64) | data formatting | bytes 1048576

commit v2 on v1

--- a/solution.py
+++ b/solution.py
@@ -51,7 +51,7 @@
         special[0:128, 128 + lane] = -np.sin(2 * np.pi * b * (lane - 63) / 128)
     r = np.arange(16)[:, None]
     twiddle = 2 * np.pi * r * b[None, :] / L
-    turn = np.stack([np.cos(twiddle), np.sin(twiddle)]).astype(np.float32)
+    turn = np.concatenate([np.cos(twiddle), np.sin(twiddle)])
 
     def near(left, right):
         return (np.abs(natural[left][:, None] - natural[right][None, :]) <= RADIUS).astype(np.float64)
@@ -62,9 +62,16 @@
     phase = 2 * np.pi * ((bins.reshape(-1)[:, None] * lag[None, :]) % L) / L
     ltable = np.concatenate([np.cos(phase), -np.sin(phase)], axis=0) / math.sqrt(NF)
     bf = ml_dtypes.bfloat16
-    bands = np.concatenate([np.concatenate([band[:256], band[256:]], axis=1), np.concatenate([band0[:128], band0[128:]], axis=1)], axis=0)
-    packed = np.concatenate([*split_table(dft), *split_table(special), bands.astype(bf)], axis=0)
-    return packed, turn, ltable.astype(bf)
+    turns = np.zeros((128, 256), bf)
+    turns[:32, :128], turns[:32, 128:] = split_table(turn)
+    rows = [
+        ltable.astype(bf),
+        np.concatenate(split_table(special), axis=1),
+        np.concatenate(split_table(dft), axis=1),
+        np.concatenate([band[128 * n : 128 * n + 128] for n in range(4)], axis=1).astype(bf),
+        np.concatenate([band0[:128].astype(bf), band0[128:].astype(bf), turns], axis=1),
+    ]
+    return np.concatenate(rows, axis=0)
 
 
 def split(values):
@@ -76,7 +83,7 @@
     return jnp.dot(left, right, preferred_element_type=F32)
 
 
-def transform(rows, tab_ref, turn_ref):
+def transform(rows, tab_ref):
     count = rows.shape[0]
     x = [rows[:, 128 * a : 128 * a + 128] for a in range(16)]
     even = [None] + [x[a] + x[16 - a] for a in range(1, 8)]
@@ -94,22 +101,23 @@
                 im = odd[a] * -s if im is None else im + odd[a] * -s
         parts_re.append(re)
         parts_im.append(im)
+    turn = tab_ref[768:800, 256:384].astype(F32) + tab_ref[768:800, 384:512].astype(F32)
     turned = []
     for r in range(1, 8):
-        c, s = turn_ref[0, r : r + 1, :], turn_ref[1, r : r + 1, :]
+        c, s = turn[r : r + 1], turn[16 + r : 17 + r]
         turned.append(jnp.concatenate([parts_re[r] * c + parts_im[r] * s, parts_im[r] * c - parts_re[r] * s], axis=1))
     y = jnp.concatenate(turned, axis=0)
-    c, s = turn_ref[0, 8:9, :], turn_ref[1, 8:9, :]
+    c, s = turn[8:9], turn[24:25]
     y0 = jnp.concatenate([parts_re[0], parts_re[8] * c, -(parts_re[8] * s)], axis=1)
 
     def product(values, at):
         high, low = split(values)
         n, depth = values.shape
-        both = dot(jnp.concatenate([high, low], axis=0), tab_ref[at : at + depth])
-        return both[:n] + both[n:] + dot(high, tab_ref[at + depth : at + 2 * depth])
-
-    spectra = product(y, 0)
-    spectra0 = product(y0, 512)
+        both = dot(jnp.concatenate([high, low], axis=0), tab_ref[at : at + depth, :256])
+        return both[:n] + both[n:] + dot(high, tab_ref[at : at + depth, 256:])
+
+    spectra = product(y, 384)
+    spectra0 = product(y0, 0)
     re = [spectra0[:, :128]] + [spectra[count * j : count * j + count, :128] for j in range(7)]
     im = [spectra0[:, 128:]] + [spectra[count * j : count * j + count, 128:] for j in range(7)]
     return re, im
@@ -131,14 +139,16 @@
     left0 = jnp.concatenate([total, amplitude[0]], axis=1)
 
     def product(values, at):
-        high, low = split(values)
-        half = values.shape[1] // 2
-        both = jnp.concatenate([high, low], axis=0)
-        both = dot(both[:, :half], tab_ref[at : at + half, :128]) + dot(both[:, half:], tab_ref[at : at + half, 128:])
-        return both[: values.shape[0]] + both[values.shape[0] :]
-
-    sums = product(left, 1280)
-    sums0 = product(left0, 1536)
+        both = jnp.concatenate(split(values), axis=0)
+        n = values.shape[0]
+        sums = dot(both[:, :128], tab_ref[at : at + 128, :128])
+        for k in range(1, values.shape[1] // 128):
+            piece = slice(128 * k, 128 * k + 128)
+            sums = sums + dot(both[:, piece], tab_ref[at : at + 128, piece])
+        return sums[:n] + sums[n:]
+
+    sums = product(left, 640)
+    sums0 = product(left0, 768)
     scale = 1.0 / (2 * RADIUS + 1)
     return [sums0 * scale] + [sums[count * j : count * j + count] * scale for j in range(7)]
 
@@ -147,14 +157,11 @@
     panel_ids_ref,
     x_hbm,
     usable_hbm,
-    tab_hbm,
-    turn_hbm,
-    lt_hbm,
+    tables_hbm,
     out_ref,
     x_ref,
     usable_ref,
     tab_ref,
-    turn_ref,
     units,
     picks,
     panel,
@@ -186,7 +193,12 @@
     loads = [
         pltpu.make_async_copy(source, target, in_sem.at[n])
         for n, (source, target) in enumerate(
-            [(x_hbm, x_ref), (turn_hbm, turn_ref), (tab_hbm, tab_ref), (usable_hbm, usable_ref), (lt_hbm, lt_ref)]
+            [
+                (x_hbm, x_ref),
+                (tables_hbm.at[pl.ds(2048, 896)], tab_ref),
+                (usable_hbm, usable_ref),
+                (tables_hbm.at[pl.ds(0, 2048)], lt_ref),
+            ]
         )
     ]
     for load in loads:
@@ -197,17 +209,36 @@
     def hello(grp, dev):
         pl.semaphore_signal(barrier, inc=1, device_id=(grp, dev), device_id_type=MESH)
 
-    def hello_grp(k, carry):
-        hello((g + k) % 16, d)
-        return carry
-
-    lax.fori_loop(1, 16, hello_grp, 0)
-
-    def hello_line(k, carry):
-        hello(2 * k + c, (1 - z_hi) * 16 + d % 16)
-        return carry
-
-    lax.fori_loop(0, 8, hello_line, 0)
+    held = 1 - (z_lo // 4 - z_hi) * (z_lo // 4 - z_hi)
+    quad = z_lo % 4
+    is_holder = held == 1
+
+    def holder_chip(side, n):
+        return side * (7 - n) + (1 - side) * n
+
+    def hello_holder(n, carry):
+        side = n // 4
+        grp, dev = holder_chip(side, n % 4) * 2 + c, side * 16 + d % 16
+
+        @pl.when((grp - g) * (grp - g) + (dev - d) * (dev - d) > 0)
+        def _():
+            hello(grp, dev)
+
+        return carry
+
+    lax.fori_loop(0, 8, hello_holder, 0)
+
+    def hello_grp(n, carry):
+        hello((g + n) % 16, d)
+        return carry
+
+    @pl.when(is_holder)
+    def _():
+        lax.fori_loop(1, 16, hello_grp, 0)
+
+    @pl.when(jnp.logical_not(is_holder))
+    def _():
+        hello(mate, d)
 
     def hello_plane(k, carry):
         hello(g, z_hi * 16 + ((xx + k) % 4) * 4 + yy)
@@ -216,10 +247,10 @@
 
     lax.fori_loop(1, 4, hello_plane, 0)
 
-    for load in loads[:4]:
+    for load in loads[:3]:
         load.wait()
     rows = jnp.concatenate([x_ref[ch].astype(F32) for ch in range(4)], axis=0)
-    spec_re, spec_im = transform(rows, tab_ref, turn_ref)
+    spec_re, spec_im = transform(rows, tab_ref)
     amplitude = [jnp.sqrt(re * re + im * im) for re, im in zip(spec_re, spec_im)]
     smooth = running_mean(amplitude, tab_ref)
 
@@ -246,23 +277,28 @@
             pair = jnp.concatenate(
                 [jnp.where(upper[t], re[8:], re[:8]), jnp.where(upper[t], im[8:], im[:8])], axis=0
             )
-            units[2 * k + t] = pair.astype(BF16)
-
-    pl.semaphore_wait(barrier, 29)
-
-    def send_unit(k, carry):
-        to = (g + k) % 16
-        pltpu.make_async_remote_copy(
-            src_ref=units.at[to],
-            dst_ref=picks.at[g],
-            send_sem=unit_send,
-            recv_sem=unit_recv,
-            device_id=(to, d),
-            device_id_type=MESH,
-        ).start()
-        return carry
-
-    lax.fori_loop(1, 16, send_unit, 0)
+            units[(k // 2) * 2 + t, k % 2] = pair.astype(BF16)
+
+    pl.semaphore_wait(barrier, 15 + 13 * held)
+
+    def send_unit(n, carry):
+        chip = holder_chip(z_hi, n // 2)
+        to = chip * 2 + n % 2
+
+        @pl.when(to != g)
+        def _():
+            pltpu.make_async_remote_copy(
+                src_ref=units.at[(chip % 4) * 2 + n % 2],
+                dst_ref=picks.at[g],
+                send_sem=unit_send,
+                recv_sem=unit_recv,
+                device_id=(to, d),
+                device_id_type=MESH,
+            ).start()
+
+        return carry
+
+    lax.fori_loop(0, 8, send_unit, 0)
     to_mate = pltpu.make_async_remote_copy(
         src_ref=own,
         dst_ref=other,
@@ -272,31 +308,41 @@
         device_id_type=MESH,
     )
     to_mate.start()
-    picks[g] = units[g]
-
-    pltpu.make_async_copy(picks.at[pl.ds(0, 15)], picks.at[pl.ds(0, 15)], unit_recv).wait()
     chosen = panel_ids_ref[c]
     owner = jnp.full((16, 128), chosen) >> 1
-    pick = jnp.where(owner == 0, picks[0].astype(F32), 0.0)
-    for k in range(1, 16):
-        pick = jnp.where(owner == k, picks[k].astype(F32), pick)
-    panel[xx, yy, z_hi, z_lo] = pick.astype(BF16)
-
-    mine = panel.at[xx, yy, z_hi, z_lo]
-
-    def send_line(k, carry):
-        z = (z_hi * 8 + z_lo + k) % 16
-        pltpu.make_async_remote_copy(
-            src_ref=mine,
-            dst_ref=mine,
-            send_sem=line_send,
-            recv_sem=line_recv,
-            device_id=((z % 8) * 2 + c, (z // 8) * 16 + d % 16),
-            device_id_type=MESH,
-        ).start()
-        return carry
-
-    lax.fori_loop(1, 16, send_line, 0)
+
+    def wait_for(ref, sem):
+        pltpu.make_async_copy(ref, ref, sem).wait()
+
+    mine = panel.at[xx, yy, z_hi, pl.ds(2 * quad, 2)]
+
+    def send_line(n, carry):
+        z = (n // 2) * (1 - n % 2) + (15 - n // 2) * (n % 2)
+        grp, dev = (z % 8) * 2 + c, (z // 8) * 16 + d % 16
+
+        @pl.when((grp - g) * (grp - g) + (dev - d) * (dev - d) > 0)
+        def _():
+            pltpu.make_async_remote_copy(
+                src_ref=mine,
+                dst_ref=mine,
+                send_sem=line_send,
+                recv_sem=line_recv.at[z_hi],
+                device_id=(grp, dev),
+                device_id_type=MESH,
+            ).start()
+
+        return carry
+
+    @pl.when(is_holder)
+    def _():
+        picks[g] = units[quad * 2 + c]
+        wait_for(picks.at[pl.ds(0, 15)], unit_recv)
+        for b in range(2):
+            pick = jnp.where(owner == 0, picks[0, b].astype(F32), 0.0)
+            for k in range(1, 16):
+                pick = jnp.where(owner == k, picks[k, b].astype(F32), pick)
+            panel[xx, yy, z_hi, 2 * quad + b] = pick.astype(BF16)
+        lax.fori_loop(0, 16, send_line, 0)
 
     low = lax.broadcasted_iota(jnp.int32, (8, 128), 0) < 4
 
@@ -335,8 +381,6 @@
     count = jnp.sum(jnp.where(match, counts, 0.0), axis=1, keepdims=True)
     scales[...] = jnp.broadcast_to(1.0 / jnp.maximum(count, 1.0), (512, 128))
 
-    pltpu.make_async_copy(picks.at[pl.ds(0, 15)], picks.at[pl.ds(0, 15)], line_recv).wait()
-
     def send_block(h, bx, by, tx, ty):
         pltpu.make_async_remote_copy(
             src_ref=panel.at[bx, by, h],
@@ -348,21 +392,39 @@
         ).start()
 
     def wait_block(h, bx, by):
-        ref = panel.at[bx, by, h]
-        pltpu.make_async_copy(ref, ref, plane_recv.at[h, bx, by]).wait()
-
-    def send_first(k, carry):
-        send_block(0, xx, yy, (xx + k) % 4, yy)
-        send_block(1, xx, yy, xx, (yy + k) % 4)
-        return carry
-
-    def send_own(k, carry):
-        send_block(0, xx, yy, xx, (yy + k) % 4)
-        send_block(1, xx, yy, (xx + k) % 4, yy)
-        return carry
-
-    lax.fori_loop(1, 4, send_first, 0)
-    lax.fori_loop(1, 4, send_own, 0)
+        wait_for(panel.at[bx, by, h], plane_recv.at[h, bx, by])
+
+    def to_x(h):
+        def send(k, carry):
+            send_block(h, xx, yy, (xx + k) % 4, yy)
+            return carry
+
+        lax.fori_loop(1, 4, send, 0)
+
+    def to_y(h):
+        def send(k, carry):
+            send_block(h, xx, yy, xx, (yy + k) % 4)
+            return carry
+
+        lax.fori_loop(1, 4, send, 0)
+
+    def wait_line(h):
+        missing = held * (1 - (z_hi - h) * (z_hi - h))
+
+        @pl.when(missing == 1)
+        def _():
+            wait_for(panel.at[0, 0, 0, pl.ds(0, 6)], line_recv.at[h])
+
+        @pl.when(missing == 0)
+        def _():
+            wait_for(panel.at[0, 0, 0], line_recv.at[h])
+
+    wait_line(0)
+    to_x(0)
+    to_y(0)
+    wait_line(1)
+    to_y(1)
+    to_x(1)
 
     def forward(k, carry):
         bx, by = (xx + k) % 4, (yy + k) % 4
@@ -390,7 +452,7 @@
     wait_block(0, xx, (yy + 1) % 4)
     wait_block(0, xx, (yy + 2) % 4)
     wait_block(0, xx, (yy + 3) % 4)
-    loads[4].wait()
+    loads[3].wait()
 
     sub = lax.broadcasted_iota(jnp.int32, (8, 128), 0)
     even1 = sub % 2 == 0
@@ -439,6 +501,16 @@
                 for i in range(2):
                     out_ref[c, s + i] = lagged[base + 4 * i : base + 4 * i + 4].astype(BF16)
                     outbox[s + i] = lagged[base + 8 + 4 * i : base + 12 + 4 * i].astype(BF16)
+        for h in range(2):
+            eight = pl.ds(h * 32 + bx * 8, 8)
+            pltpu.make_async_remote_copy(
+                src_ref=outbox.at[eight],
+                dst_ref=out_ref.at[c, eight],
+                send_sem=out_send,
+                recv_sem=out_recv,
+                device_id=(mate, d),
+                device_id_type=MESH,
+            ).start()
         return carry
 
     quarter(0, 0)
@@ -457,44 +529,37 @@
 
     lax.fori_loop(1, 4, later, 0)
 
-    to_out = pltpu.make_async_remote_copy(
-        src_ref=outbox,
-        dst_ref=out_ref.at[c],
-        send_sem=out_send,
-        recv_sem=out_recv,
-        device_id=(mate, d),
-        device_id_type=MESH,
-    )
-    to_out.start()
-
-    pltpu.make_async_copy(picks.at[pl.ds(0, 15)], picks.at[pl.ds(0, 15)], unit_send).wait()
-    pltpu.make_async_copy(picks.at[pl.ds(0, 15)], picks.at[pl.ds(0, 15)], line_send).wait()
+    @pl.when(is_holder)
+    def _():
+        wait_for(picks.at[pl.ds(0, 7)], unit_send)
+        wait_for(picks.at[pl.ds(0, 15)], line_send)
+
+    @pl.when(jnp.logical_not(is_holder))
+    def _():
+        wait_for(picks.at[pl.ds(0, 8)], unit_send)
+
     to_mate.wait_send()
     for part in range(3):
-        ref = panel.at[part]
-        pltpu.make_async_copy(ref, ref, plane_send).wait()
-    ref = panel.at[3, pl.ds(0, 3)]
-    pltpu.make_async_copy(ref, ref, plane_send).wait()
-    to_out.wait_send()
-    pltpu.make_async_copy(outbox, outbox, out_recv).wait()
+        wait_for(panel.at[part], plane_send)
+    wait_for(panel.at[3, pl.ds(0, 3)], plane_send)
+    wait_for(outbox, out_send)
+    wait_for(outbox, out_recv)
 
 
 def on_device(records, usable, panel_ids):
-    tables = [jnp.asarray(t) for t in make_tables()]
     vmem = pl.BlockSpec(memory_space=pltpu.VMEM)
     dma = pltpu.SemaphoreType.DMA
     return pl.pallas_call(
         kernel,
         out_shape=jax.ShapeDtypeStruct((2, 64, 4, NLAG), BF16),
-        in_specs=[pl.BlockSpec(memory_space=pltpu.SMEM)] + [pl.BlockSpec(memory_space=pltpu.HBM)] * 5,
+        in_specs=[pl.BlockSpec(memory_space=pltpu.SMEM)] + [pl.BlockSpec(memory_space=pltpu.HBM)] * 3,
         out_specs=vmem,
         scratch_shapes=[
             pltpu.VMEM((4, 4, 2048), BF16),
             pltpu.VMEM((4, 2048), jnp.int32),
-            pltpu.VMEM((1664, 256), BF16),
-            pltpu.VMEM((2, 16, 128), F32),
-            pltpu.VMEM((16, 16, 128), BF16),
-            pltpu.VMEM((16, 16, 128), BF16),
+            pltpu.VMEM((896, 512), BF16),
+            pltpu.VMEM((8, 2, 16, 128), BF16),
+            pltpu.VMEM((16, 2, 16, 128), BF16),
             pltpu.VMEM((4, 4, 2, 8, 16, 128), BF16),
             pltpu.VMEM((16, 16, 128), BF16),
             pltpu.VMEM((16, 16, 128), BF16),
@@ -503,22 +568,22 @@
             pltpu.VMEM((2048, NLAG), BF16),
             pltpu.VMEM((512, 128), F32),
             pltpu.VMEM((64, 4, NLAG), BF16),
-            dma((5,)),
-            dma,
-            dma,
-            dma,
-            dma,
-            dma,
-            dma,
+            dma((4,)),
+            dma,
+            dma,
+            dma,
+            dma,
+            dma,
+            dma((2,)),
             dma,
             dma((2, 4, 4)),
             dma,
             dma,
         ],
         compiler_params=pltpu.CompilerParams(
-            collective_id=0, has_side_effects=True, vmem_limit_bytes=60 * 1024 * 1024
+            collective_id=0, has_side_effects=True, vmem_limit_bytes=52 * 1024 * 1024
         ),
-    )(panel_ids, records, usable.T, *tables)
+    )(*[pltpu.with_memory_space_constraint(a, pltpu.HBM) for a in (panel_ids, records, usable.T, jnp.asarray(make_tables()))])
 
 
 def solution(mesh):

time: 49 us -> 44.4 us (0.906)
  Pallas kernels: 46.8 us -> 43.4 us
  local copies, waits for them, and re-layouts: 2.02 us -> 0.8 us
    pallas_call x1, Pallas kernels: 46.8 us -> 43.4 us  [on_device(): pl.pallas_call(kernel, out_shape=jax.ShapeDtypeStruct((2, 64, 4, NLAG), B...]
    unnamed x1, local copies, waits for them, and re-layouts: 2.02 us -> 0.8 us
where the time goes in v2:
time: 44.4 us; the launch traced here: 44.2 us
  Pallas kernels  43.4 us (98%)
  local copies, waits for them, and re-layouts  0.8 us (2%)
    pallas_call x1, Pallas kernels, on_device(): pl.pallas_call(kernel, out_shape=jax.ShapeDtypeStruct((2, 64, 4, NLAG), B...  43.4 us

profile of v2, /device:TPU:1, one launch (start us, length us, event | category | flops | bytes accessed | tf_op | source)
XLA Modules:
  0.0 44.2 jit_solution(8777363216239989926)
XLA Ops:
  0.0 43.4 %shard_map.46 = bf16[2,64,4,512]{3,2,1,0:T(4,128)(2,1)S(1)} custom-call(s32[2]{0:T(128)} %panel_ids_ref.1, bf16[4,4,2048]{2,1,0:T(4,128)(2,1)} %x_hbm.1, s32[4,2048]{1,0:T(4,128)} %bitcast.1, bf16[2944,512]{1,0:T(8,128)(2,1)} %constant.2.clone.tables_hbm), custom_call_target="tpu_custom_call" | custom-call | tf_op jit(solution)/shard_map/pallas_call | solution.py:552
  43.4 0.8 %copy.6 = bf16[2,64,4,512]{3,2,1,0:T(4,128)(2,1)} copy(bf16[2,64,4,512]{3,2,1,0:T(4,128)(2,1)S(1)} %shard_map.46) | data formatting | bytes 1048576

commit v3 on v2

--- a/solution.py
+++ b/solution.py
@@ -13,6 +13,8 @@
 NF = 1024
 RADIUS = 64
 NLAG = 512
+FIRST = 12
+SECOND = 22
 F32 = jnp.float32
 BF16 = jnp.bfloat16
 MESH = pl.DeviceIdType.MESH
@@ -169,6 +171,7 @@
     other,
     recv,
     lhs,
+    lagged,
     lt_ref,
     scales,
     outbox,
@@ -179,6 +182,7 @@
     other_recv,
     line_send,
     line_recv,
+    relay_send,
     plane_send,
     plane_recv,
     out_send,
@@ -216,17 +220,30 @@
     def holder_chip(side, n):
         return side * (7 - n) + (1 - side) * n
 
+    zz = z_hi * 8 + z_lo
+    is_far = z_hi * (1 - z_lo // 4) == 1
+    is_relay = (zz - 7) * (zz - 12) == 0
+
+    def line_device(z):
+        return (z % 8) * 2 + c, (z // 8) * 16 + d % 16
+
     def hello_holder(n, carry):
         side = n // 4
-        grp, dev = holder_chip(side, n % 4) * 2 + c, side * 16 + d % 16
-
-        @pl.when((grp - g) * (grp - g) + (dev - d) * (dev - d) > 0)
-        def _():
-            hello(grp, dev)
+        z = side * 8 + holder_chip(side, n % 4)
+
+        @pl.when(z != zz)
+        def _():
+            hello(*line_device(z))
 
         return carry
 
-    lax.fori_loop(0, 8, hello_holder, 0)
+    @pl.when(jnp.logical_not(is_far))
+    def _():
+        lax.fori_loop(0, 8, hello_holder, 0)
+
+    @pl.when(is_far)
+    def _():
+        hello(*line_device(7 + 5 * ((zz - 8) // 2)))
 
     def hello_grp(n, carry):
         hello((g + n) % 16, d)
@@ -240,16 +257,19 @@
     def _():
         hello(mate, d)
 
-    def hello_plane(k, carry):
-        hello(g, z_hi * 16 + ((xx + k) % 4) * 4 + yy)
-        hello(g, z_hi * 16 + xx * 4 + (yy + k) % 4)
+    def hello_plane(n, carry):
+        i, j = 2 - n // 4 + 3 * (n // 8) - 2 * (n // 12), 2 - n % 4 + 3 * ((n % 4) // 2) - 2 * ((n % 4) // 3)
+        hello(g, z_hi * 16 + ((xx + i) % 4) * 4 + (yy + j) % 4)
         return carry
 
-    lax.fori_loop(1, 4, hello_plane, 0)
+    lax.fori_loop(0, 15, hello_plane, 0)
 
     for load in loads[:3]:
         load.wait()
-    rows = jnp.concatenate([x_ref[ch].astype(F32) for ch in range(4)], axis=0)
+    loaded = [x_ref[ch].astype(F32) for ch in range(4)]
+    rows = jnp.concatenate(
+        [loaded[2 * pair + i][w : w + 1] for pair in range(2) for w in range(4) for i in range(2)], axis=0
+    )
     spec_re, spec_im = transform(rows, tab_ref)
     amplitude = [jnp.sqrt(re * re + im * im) for re, im in zip(spec_re, spec_im)]
     smooth = running_mean(amplitude, tab_ref)
@@ -257,10 +277,13 @@
     lane16 = lax.broadcasted_iota(jnp.int32, (16, 128), 1)
     row16 = lax.broadcasted_iota(jnp.int32, (16, 128), 0)
 
+    def twice(block):
+        return jnp.concatenate([block[w // 2 : w // 2 + 1] for w in range(8)], axis=0)
+
     def mask_of(group):
         block = usable_ref[:, pl.ds(pl.multiple_of(group * 128, 128), 128)].astype(F32)
-        tiled = jnp.concatenate([block] * 4, axis=0)
-        chosen = jnp.where(lane16 == 4 * d + row16 // 4, tiled, 0.0)
+        tiled = jnp.concatenate([twice(block)] * 2, axis=0)
+        chosen = jnp.where(lane16 == 4 * d + (row16 // 8) * 2 + row16 % 2, tiled, 0.0)
         return jnp.sum(chosen, axis=1, keepdims=True)
 
     own_mask = mask_of(g)
@@ -279,7 +302,14 @@
             )
             units[(k // 2) * 2 + t, k % 2] = pair.astype(BF16)
 
-    pl.semaphore_wait(barrier, 15 + 13 * held)
+    @pl.when(is_relay)
+    def _():
+        pl.semaphore_wait(barrier, 26 + 9 * held)
+
+    @pl.when(jnp.logical_not(is_relay))
+    def _():
+        pl.semaphore_wait(barrier, 24 + 9 * held)
+
 
     def send_unit(n, carry):
         chip = holder_chip(z_hi, n // 2)
@@ -311,6 +341,43 @@
     chosen = panel_ids_ref[c]
     owner = jnp.full((16, 128), chosen) >> 1
 
+    sub = lax.broadcasted_iota(jnp.int32, (8, 128), 0)
+    first_of_pair = sub % 2 == 0
+
+    def spread(side, source):
+        def one(p, carry):
+            tile = source[p].astype(F32)
+            for pair in range(2):
+                rows8 = tile[8 * pair : 8 * pair + 8]
+                recv[side, p, 2 * pair] = jnp.where(first_of_pair, rows8, pltpu.roll(rows8, 1, 0))
+                recv[side, p, 2 * pair + 1] = jnp.where(first_of_pair, pltpu.roll(rows8, 7, 0), rows8)
+            return carry
+
+        lax.fori_loop(0, 16, one, 0)
+
+    spread(0, own)
+    to_mate.wait_recv()
+    spread(1, other)
+
+    block = usable_ref[:, :128]
+    for k in range(1, 16):
+        block = jnp.where(owner[:4] == k, usable_ref[:, 128 * k : 128 * k + 128], block)
+    block = block.astype(F32)
+    weights = jnp.concatenate([twice(block)] * 4, axis=0) * jnp.concatenate([own_mask, mate_mask], axis=0)
+    row = lax.broadcasted_iota(jnp.int32, (512, 128), 0)
+    lane = lax.broadcasted_iota(jnp.int32, (512, 128), 1)
+    at_x = (xx + row // 128) % 4
+    at_y = (yy + (row // 32) % 4) % 4
+    at_dev = ((row // 16) % 2) * 16 + at_x * 4 + at_y
+    half = jnp.full((512, 128), chosen) & 1
+    picked = jnp.where(lane == at_dev * 4 + half * 2 + row % 2, 1.0, 0.0).astype(BF16)
+    counts = lax.dot_general(picked, weights.astype(BF16), (((1,), (1,)), ((), ())), preferred_element_type=F32)
+    row32 = lax.broadcasted_iota(jnp.int32, (512, 32), 0)
+    lane32 = lax.broadcasted_iota(jnp.int32, (512, 32), 1)
+    match = (lane32 // 8) * 2 + lane32 % 2 == ((row32 // 8) % 2) * 4 + (row32 // 2) % 4
+    count = jnp.sum(jnp.where(match, counts, 0.0), axis=1, keepdims=True)
+    scales[...] = jnp.broadcast_to(1.0 / jnp.maximum(count, 1.0), (512, 128))
+
     def wait_for(ref, sem):
         pltpu.make_async_copy(ref, ref, sem).wait()
 
@@ -318,16 +385,16 @@
 
     def send_line(n, carry):
         z = (n // 2) * (1 - n % 2) + (15 - n // 2) * (n % 2)
-        grp, dev = (z % 8) * 2 + c, (z // 8) * 16 + d % 16
-
-        @pl.when((grp - g) * (grp - g) + (dev - d) * (dev - d) > 0)
+        z = z - 4 * ((n // 8) * (n % 2))
+
+        @pl.when(z != zz)
         def _():
             pltpu.make_async_remote_copy(
                 src_ref=mine,
                 dst_ref=mine,
                 send_sem=line_send,
                 recv_sem=line_recv.at[z_hi],
-                device_id=(grp, dev),
+                device_id=line_device(z),
                 device_id_type=MESH,
             ).start()
 
@@ -342,71 +409,7 @@
             for k in range(1, 16):
                 pick = jnp.where(owner == k, picks[k, b].astype(F32), pick)
             panel[xx, yy, z_hi, 2 * quad + b] = pick.astype(BF16)
-        lax.fori_loop(0, 16, send_line, 0)
-
-    low = lax.broadcasted_iota(jnp.int32, (8, 128), 0) < 4
-
-    def spread(side, source):
-        def one(p, carry):
-            tile = source[p].astype(F32)
-            for pair in range(2):
-                rows8 = tile[8 * pair : 8 * pair + 8]
-                turned = pltpu.roll(rows8, 4, 0)
-                recv[side, p, 2 * pair] = jnp.where(low, rows8, turned)
-                recv[side, p, 2 * pair + 1] = jnp.where(low, turned, rows8)
-            return carry
-
-        lax.fori_loop(0, 16, one, 0)
-
-    spread(0, own)
-    to_mate.wait_recv()
-    spread(1, other)
-
-    block = usable_ref[:, :128]
-    for k in range(1, 16):
-        block = jnp.where(owner[:4] == k, usable_ref[:, 128 * k : 128 * k + 128], block)
-    block = block.astype(F32)
-    weights = jnp.concatenate([block] * 8, axis=0) * jnp.concatenate([own_mask, mate_mask], axis=0)
-    row = lax.broadcasted_iota(jnp.int32, (512, 128), 0)
-    lane = lax.broadcasted_iota(jnp.int32, (512, 128), 1)
-    at_x = (xx + row // 128) % 4
-    at_y = (yy + (row // 32) % 4) % 4
-    at_dev = ((row // 16) % 2) * 16 + at_x * 4 + at_y
-    half = jnp.full((512, 128), chosen) & 1
-    picked = jnp.where(lane == at_dev * 4 + half * 2 + (row // 4) % 2, 1.0, 0.0).astype(BF16)
-    counts = lax.dot_general(picked, weights.astype(BF16), (((1,), (1,)), ((), ())), preferred_element_type=F32)
-    row32 = lax.broadcasted_iota(jnp.int32, (512, 32), 0)
-    lane32 = lax.broadcasted_iota(jnp.int32, (512, 32), 1)
-    match = lane32 // 4 == ((row32 // 8) % 2) * 4 + row32 % 4
-    count = jnp.sum(jnp.where(match, counts, 0.0), axis=1, keepdims=True)
-    scales[...] = jnp.broadcast_to(1.0 / jnp.maximum(count, 1.0), (512, 128))
-
-    def send_block(h, bx, by, tx, ty):
-        pltpu.make_async_remote_copy(
-            src_ref=panel.at[bx, by, h],
-            dst_ref=panel.at[bx, by, h],
-            send_sem=plane_send,
-            recv_sem=plane_recv.at[h, bx, by],
-            device_id=(g, z_hi * 16 + tx * 4 + ty),
-            device_id_type=MESH,
-        ).start()
-
-    def wait_block(h, bx, by):
-        wait_for(panel.at[bx, by, h], plane_recv.at[h, bx, by])
-
-    def to_x(h):
-        def send(k, carry):
-            send_block(h, xx, yy, (xx + k) % 4, yy)
-            return carry
-
-        lax.fori_loop(1, 4, send, 0)
-
-    def to_y(h):
-        def send(k, carry):
-            send_block(h, xx, yy, xx, (yy + k) % 4)
-            return carry
-
-        lax.fori_loop(1, 4, send, 0)
+        lax.fori_loop(0, 12, send_line, 0)
 
     def wait_line(h):
         missing = held * (1 - (z_hi - h) * (z_hi - h))
@@ -419,52 +422,76 @@
         def _():
             wait_for(panel.at[0, 0, 0], line_recv.at[h])
 
+        def relay(n, carry):
+            ref = panel.at[xx, yy, h]
+            pltpu.make_async_remote_copy(
+                src_ref=ref,
+                dst_ref=ref,
+                send_sem=relay_send,
+                recv_sem=line_recv.at[h],
+                device_id=line_device(8 + n + z_hi * (3 - 2 * n)),
+                device_id_type=MESH,
+            ).start()
+            return carry
+
+        @pl.when(is_relay)
+        def _():
+            lax.fori_loop(0, 2, relay, 0)
+
+    def offset(n):
+        return 2 - n + 3 * (n // 2) - 2 * (n // 3)
+
+    def place_of(h, n):
+        i, j = offset(n // 4), offset(n % 4)
+        return i * (1 - h) + j * h, j * (1 - h) + i * h
+
+    def to_plane(h):
+        ref = panel.at[xx, yy, h]
+
+        def start(tx, ty):
+            pltpu.make_async_remote_copy(
+                src_ref=ref,
+                dst_ref=ref,
+                send_sem=plane_send,
+                recv_sem=plane_recv.at[h, xx, yy],
+                device_id=(g, z_hi * 16 + tx * 4 + ty),
+                device_id_type=MESH,
+            ).start()
+
+        @pl.when(xx + yy > 0)
+        def _():
+            start(0, 0)
+
+        def send(n, carry):
+            dx, dy = place_of(h, n)
+            tx, ty = (xx + dx) % 4, (yy + dy) % 4
+
+            @pl.when(tx + ty > 0)
+            def _():
+                start(tx, ty)
+
+            return carry
+
+        lax.fori_loop(0, 15, send, 0)
+
     wait_line(0)
-    to_x(0)
-    to_y(0)
+    to_plane(0)
     wait_line(1)
-    to_y(1)
-    to_x(1)
-
-    def forward(k, carry):
-        bx, by = (xx + k) % 4, (yy + k) % 4
-        wait_block(0, bx, yy)
-
-        def on_y(m, inner):
-            send_block(0, bx, yy, xx, (yy + m) % 4)
-            return inner
-
-        lax.fori_loop(1, 4, on_y, 0)
-        wait_block(1, xx, by)
-
-        def on_x(m, inner):
-            send_block(1, xx, by, (xx + m) % 4, yy)
-            return inner
-
-        lax.fori_loop(1, 4, on_x, 0)
-        return carry
-
-    lax.fori_loop(1, 4, forward, 0)
-
-    wait_block(1, (xx + 1) % 4, yy)
-    wait_block(1, (xx + 2) % 4, yy)
-    wait_block(1, (xx + 3) % 4, yy)
-    wait_block(0, xx, (yy + 1) % 4)
-    wait_block(0, xx, (yy + 2) % 4)
-    wait_block(0, xx, (yy + 3) % 4)
-    loads[3].wait()
-
-    sub = lax.broadcasted_iota(jnp.int32, (8, 128), 0)
-    even1 = sub % 2 == 0
-    even2 = (sub // 2) % 2 == 0
+    to_plane(1)
+
+    window = sub // 2
+    lower = window < 2
+    inner_two = (window == 1) | (window == 2)
+    even = window % 2 == 0
 
     def fold(v):
-        first = jnp.where(even1, v[0] + pltpu.roll(v[0], 7, 0), v[1] + pltpu.roll(v[1], 1, 0))
-        second = jnp.where(even1, v[2] + pltpu.roll(v[2], 7, 0), v[3] + pltpu.roll(v[3], 1, 0))
-        return jnp.where(even2, first + pltpu.roll(first, 6, 0), second + pltpu.roll(second, 2, 0))
-
-    def cross(line, bx, by, h):
-        slot = line * 2 + h
+        u = jnp.where(lower, v[0], v[2]) + pltpu.roll(jnp.where(lower, v[2], v[0]), 4, 0)
+        t = jnp.where(inner_two, v[1], v[3]) + pltpu.roll(jnp.where(inner_two, v[3], v[1]), 4, 0)
+        return jnp.where(even, u, t) + pltpu.roll(jnp.where(even, t, u), 6, 0)
+
+    def cross(slot, h, dx, dy):
+        bx, by = (xx + dx) % 4, (yy + dy) % 4
+        at = pl.ds(pl.multiple_of(slot * 16, 16), 16)
         for k in range(8):
             both = panel[bx, by, h, k].astype(F32)
             a, b = both[:8], both[8:]
@@ -477,66 +504,72 @@
                     im.append(b * cc - a * ee)
                 re_rows.append(fold(re))
                 im_rows.append(fold(im))
-            at = pl.ds(pl.multiple_of(slot * 16, 16), 16)
             lhs[at, 128 * k : 128 * k + 128] = jnp.concatenate(re_rows, axis=0).astype(BF16)
             lhs[at, 1024 + 128 * k : 1152 + 128 * k] = jnp.concatenate(im_rows, axis=0).astype(BF16)
 
-    def quarter(q, carry):
-        bx = (xx + q) % 4
-
-        def one_line(m, inner):
-            by = (yy + m) % 4
-            cross(q * 4 + m, bx, by, 0)
-            cross(q * 4 + m, bx, by, 1)
-            return inner
-
-        lax.fori_loop(0, 4, one_line, 0)
-        at = pl.ds(pl.multiple_of(q * 128, 128), 128)
-        lagged = dot(lhs[at, :], lt_ref[...]) * jnp.concatenate([scales[at, :]] * 4, axis=1)
-        for m in range(4):
-            by = (yy + m) % 4
-            for h in range(2):
-                base = m * 32 + h * 16
-                s = (h * 16 + bx * 4 + by) * 2
-                for i in range(2):
-                    out_ref[c, s + i] = lagged[base + 4 * i : base + 4 * i + 4].astype(BF16)
-                    outbox[s + i] = lagged[base + 8 + 4 * i : base + 12 + 4 * i].astype(BF16)
-        for h in range(2):
-            eight = pl.ds(h * 32 + bx * 8, 8)
+    def finish(first, many, place):
+        rows = pl.ds(pl.multiple_of(first * 16, 16), many * 16)
+        lagged[: many * 16] = dot(lhs[rows, :], lt_ref[...])
+
+        def one(n, carry):
+            h, dx, dy = place(n)
+            s = (h * 16 + ((xx + dx) % 4) * 4 + (yy + dy) % 4) * 2
+            scale = scales[pl.ds(pl.multiple_of((dx * 8 + dy * 2 + h) * 16, 16), 16), :]
+            slot_rows = pl.ds(pl.multiple_of(n * 16, 16), 16)
+            values = lagged[slot_rows, :] * jnp.concatenate([scale] * 4, axis=1)
+            out_rows = [jnp.concatenate([values[at + 2 * r : at + 2 * r + 1] for r in range(4)], axis=0) for at in (0, 1, 8, 9)]
+            for i in range(2):
+                out_ref[c, s + i] = out_rows[i].astype(BF16)
+                outbox[s + i] = out_rows[2 + i].astype(BF16)
+            pair = pl.ds(s, 2)
             pltpu.make_async_remote_copy(
-                src_ref=outbox.at[eight],
-                dst_ref=out_ref.at[c, eight],
+                src_ref=outbox.at[pair],
+                dst_ref=out_ref.at[c, pair],
                 send_sem=out_send,
                 recv_sem=out_recv,
                 device_id=(mate, d),
                 device_id_type=MESH,
             ).start()
+            return carry
+
+        lax.fori_loop(0, many, one, 0)
+
+    def place(slot):
+        h, n = slot // 16, (slot + 15) % 16
+        dx, dy = place_of(h, n)
+        return h, (4 - dx) % 4, (4 - dy) % 4
+
+    def arrive(slot, carry):
+        h, dx, dy = place(slot)
+        bx, by = (xx + dx) % 4, (yy + dy) % 4
+
+        @pl.when(slot % 16 > 0)
+        def _():
+            wait_for(panel.at[bx, by, h], plane_recv.at[h, bx, by])
+
+        cross(slot, h, dx, dy)
         return carry
 
-    quarter(0, 0)
-
-    def later(q, carry):
-        bx = (xx + q) % 4
-
-        def wait_line(m, inner):
-            by = (yy + m) % 4
-            wait_block(0, bx, by)
-            wait_block(1, bx, by)
-            return inner
-
-        lax.fori_loop(1, 4, wait_line, 0)
-        return quarter(q, carry)
-
-    lax.fori_loop(1, 4, later, 0)
+    lax.fori_loop(0, FIRST, arrive, 0)
+    loads[3].wait()
+    finish(0, FIRST, place)
+    lax.fori_loop(FIRST, SECOND, arrive, 0)
+    finish(FIRST, SECOND - FIRST, lambda n: place(n + FIRST))
+    lax.fori_loop(SECOND, 32, arrive, 0)
+    finish(SECOND, 32 - SECOND, lambda n: place(n + SECOND))
 
     @pl.when(is_holder)
     def _():
         wait_for(picks.at[pl.ds(0, 7)], unit_send)
-        wait_for(picks.at[pl.ds(0, 15)], line_send)
+        wait_for(picks.at[pl.ds(0, 11)], line_send)
 
     @pl.when(jnp.logical_not(is_holder))
     def _():
         wait_for(picks.at[pl.ds(0, 8)], unit_send)
+
+    @pl.when(is_relay)
+    def _():
+        wait_for(panel.at[0, pl.ds(0, 2)], relay_send)
 
     to_mate.wait_send()
     for part in range(3):
@@ -565,6 +598,7 @@
             pltpu.VMEM((16, 16, 128), BF16),
             pltpu.VMEM((2, 16, 4, 8, 128), F32),
             pltpu.VMEM((512, 2048), BF16),
+            pltpu.VMEM((320, NLAG), F32),
             pltpu.VMEM((2048, NLAG), BF16),
             pltpu.VMEM((512, 128), F32),
             pltpu.VMEM((64, 4, NLAG), BF16),
@@ -575,6 +609,7 @@
             dma,
             dma,
             dma((2,)),
+            dma,
             dma,
             dma((2, 4, 4)),
             dma,

time: 44.4 us -> 44.3 us (level)
  no operation moved by 1% of the time
where the time goes in v3:
time: 44.3 us; the launch traced here: 44.2 us
  Pallas kernels  43.4 us (98%)
  local copies, waits for them, and re-layouts  0.8 us (2%)
    pallas_call x1, Pallas kernels, on_device(): pl.pallas_call(kernel, out_shape=jax.ShapeDtypeStruct((2, 64, 4, NLAG), B...  43.4 us

profile of v3, /device:TPU:1, one launch (start us, length us, event | category | flops | bytes accessed | tf_op | source)
XLA Modules:
  0.0 44.2 jit_solution(1856891086566126355)
XLA Ops:
  0.0 43.4 %shard_map.46 = bf16[2,64,4,512]{3,2,1,0:T(4,128)(2,1)S(1)} custom-call(s32[2]{0:T(128)} %panel_ids_ref.1, bf16[4,4,2048]{2,1,0:T(4,128)(2,1)} %x_hbm.1, s32[4,2048]{1,0:T(4,128)} %bitcast.1, bf16[2944,512]{1,0:T(8,128)(2,1)} %constant.2.clone.tables_hbm), custom_call_target="tpu_custom_call" | custom-call | tf_op jit(solution)/shard_map/pallas_call | solution.py:585
  43.4 0.8 %copy.6 = bf16[2,64,4,512]{3,2,1,0:T(4,128)(2,1)} copy(bf16[2,64,4,512]{3,2,1,0:T(4,128)(2,1)S(1)} %shard_map.46) | data formatting | bytes 1048576

commit v4 on v3

--- a/solution.py
+++ b/solution.py
@@ -13,8 +13,6 @@
 NF = 1024
 RADIUS = 64
 NLAG = 512
-FIRST = 12
-SECOND = 22
 F32 = jnp.float32
 BF16 = jnp.bfloat16
 MESH = pl.DeviceIdType.MESH
@@ -257,12 +255,12 @@
     def _():
         hello(mate, d)
 
-    def hello_plane(n, carry):
-        i, j = 2 - n // 4 + 3 * (n // 8) - 2 * (n // 12), 2 - n % 4 + 3 * ((n % 4) // 2) - 2 * ((n % 4) // 3)
-        hello(g, z_hi * 16 + ((xx + i) % 4) * 4 + (yy + j) % 4)
-        return carry
-
-    lax.fori_loop(0, 15, hello_plane, 0)
+    def hello_plane(k, carry):
+        hello(g, z_hi * 16 + ((xx + k) % 4) * 4 + yy)
+        hello(g, z_hi * 16 + xx * 4 + (yy + k) % 4)
+        return carry
+
+    lax.fori_loop(1, 4, hello_plane, 0)
 
     for load in loads[:3]:
         load.wait()
@@ -304,11 +302,11 @@
 
     @pl.when(is_relay)
     def _():
-        pl.semaphore_wait(barrier, 26 + 9 * held)
+        pl.semaphore_wait(barrier, 17 + 9 * held)
 
     @pl.when(jnp.logical_not(is_relay))
     def _():
-        pl.semaphore_wait(barrier, 24 + 9 * held)
+        pl.semaphore_wait(barrier, 15 + 9 * held)
 
 
     def send_unit(n, carry):
@@ -438,46 +436,65 @@
         def _():
             lax.fori_loop(0, 2, relay, 0)
 
-    def offset(n):
-        return 2 - n + 3 * (n // 2) - 2 * (n // 3)
-
-    def place_of(h, n):
-        i, j = offset(n // 4), offset(n % 4)
-        return i * (1 - h) + j * h, j * (1 - h) + i * h
-
-    def to_plane(h):
-        ref = panel.at[xx, yy, h]
-
-        def start(tx, ty):
-            pltpu.make_async_remote_copy(
-                src_ref=ref,
-                dst_ref=ref,
-                send_sem=plane_send,
-                recv_sem=plane_recv.at[h, xx, yy],
-                device_id=(g, z_hi * 16 + tx * 4 + ty),
-                device_id_type=MESH,
-            ).start()
-
-        @pl.when(xx + yy > 0)
-        def _():
-            start(0, 0)
-
+    def send_block(h, u, bx, by, tx, ty):
+        ref = panel.at[bx, by, h, pl.ds(4 * u, 4)]
+        pltpu.make_async_remote_copy(
+            src_ref=ref,
+            dst_ref=ref,
+            send_sem=plane_send,
+            recv_sem=plane_recv.at[h, u, bx, by],
+            device_id=(g, z_hi * 16 + tx * 4 + ty),
+            device_id_type=MESH,
+        ).start()
+
+    def wait_block(h, u, bx, by):
+        wait_for(panel.at[bx, by, h, pl.ds(4 * u, 4)], plane_recv.at[h, u, bx, by])
+
+    def distance(n):
+        return 1 + 2 * (n % 2) + n // 2
+
+    def others(n, own_place):
+        return n + (n + 4 - own_place) // 4
+
+    def to_x(h):
         def send(n, carry):
-            dx, dy = place_of(h, n)
-            tx, ty = (xx + dx) % 4, (yy + dy) % 4
-
-            @pl.when(tx + ty > 0)
-            def _():
-                start(tx, ty)
-
+            send_block(h, n // 3, xx, yy, others(n % 3, xx), yy)
             return carry
 
-        lax.fori_loop(0, 15, send, 0)
+        lax.fori_loop(0, 6, send, 0)
+
+    def to_y(h):
+        def send(n, carry):
+            send_block(h, n // 3, xx, yy, xx, others(n % 3, yy))
+            return carry
+
+        lax.fori_loop(0, 6, send, 0)
 
     wait_line(0)
-    to_plane(0)
+    to_x(0)
     wait_line(1)
-    to_plane(1)
+    to_y(1)
+    to_y(0)
+    to_x(1)
+
+    def forward(n, carry):
+        u, k = n % 2, distance(n // 2)
+        bx, by = (xx + k) % 4, (yy + k) % 4
+        wait_block(0, u, bx, yy)
+
+        def on_y(m, inner):
+            send_block(0, u, bx, yy, xx, others(m, yy))
+            return inner
+
+        lax.fori_loop(0, 3, on_y, 0)
+        wait_block(1, u, xx, by)
+
+        def on_x(m, inner):
+            send_block(1, u, xx, by, others(m, xx), yy)
+            return inner
+
+        lax.fori_loop(0, 3, on_x, 0)
+        return carry
 
     window = sub // 2
     lower = window < 2
@@ -534,29 +551,60 @@
 
         lax.fori_loop(0, many, one, 0)
 
-    def place(slot):
-        h, n = slot // 16, (slot + 15) % 16
-        dx, dy = place_of(h, n)
-        return h, (4 - dx) % 4, (4 - dy) % 4
-
-    def arrive(slot, carry):
-        h, dx, dy = place(slot)
-        bx, by = (xx + dx) % 4, (yy + dy) % 4
-
-        @pl.when(slot % 16 > 0)
-        def _():
-            wait_for(panel.at[bx, by, h], plane_recv.at[h, bx, by])
-
-        cross(slot, h, dx, dy)
-        return carry
-
-    lax.fori_loop(0, FIRST, arrive, 0)
+    def first_place(n):
+        k, axis, h = distance(n // 4), (n // 2) % 2, n % 2
+        return h, k * (1 - axis), k * axis
+
+    def cross_own(h, carry):
+        cross(h, h, 0, 0)
+        return carry
+
+    lax.fori_loop(0, 2, cross_own, 0)
+
+    def cross_first(n, carry):
+        h, dx, dy = first_place(n)
+
+        @pl.when(dx * (1 - h) + dy * h == 0)
+        def _():
+            wait_block(h, 0, (xx + dx) % 4, (yy + dy) % 4)
+            wait_block(h, 1, (xx + dx) % 4, (yy + dy) % 4)
+
+        cross(n + 2, h, dx, dy)
+        return carry
+
+    def forward_and_cross(n, carry):
+        forward(n, carry)
+
+        @pl.when(n % 2 == 1)
+        def _():
+            lax.fori_loop(0, 2, lambda m, inner: cross_first(4 * (n // 2) + 3 * m, inner), 0)
+
+        return carry
+
+    lax.fori_loop(0, 6, forward_and_cross, 0)
+    lax.fori_loop(0, 6, lambda n, inner: cross_first(4 * (n // 2) + 1 + n % 2, inner), 0)
     loads[3].wait()
-    finish(0, FIRST, place)
-    lax.fori_loop(FIRST, SECOND, arrive, 0)
-    finish(FIRST, SECOND - FIRST, lambda n: place(n + FIRST))
-    lax.fori_loop(SECOND, 32, arrive, 0)
-    finish(SECOND, 32 - SECOND, lambda n: place(n + SECOND))
+
+    def early_place(n):
+        h, dx, dy = first_place(n - 2 * jnp.minimum(n // 2, 1))
+        later = jnp.minimum(n // 2, 1)
+        return h, dx * later, dy * later
+
+    finish(0, 14, early_place)
+
+    def second_place(n):
+        k, m, h = distance(n // 6), distance((n // 2) % 3), n % 2
+        return h, k * (1 - h) + m * h, m * (1 - h) + k * h
+
+    def cross_second(n, carry):
+        h, dx, dy = second_place(n)
+        wait_block(h, 0, (xx + dx) % 4, (yy + dy) % 4)
+        wait_block(h, 1, (xx + dx) % 4, (yy + dy) % 4)
+        cross(14 + n, h, dx, dy)
+        return carry
+
+    lax.fori_loop(0, 18, cross_second, 0)
+    finish(14, 18, second_place)
 
     @pl.when(is_holder)
     def _():
@@ -598,7 +646,7 @@
             pltpu.VMEM((16, 16, 128), BF16),
             pltpu.VMEM((2, 16, 4, 8, 128), F32),
             pltpu.VMEM((512, 2048), BF16),
-            pltpu.VMEM((320, NLAG), F32),
+            pltpu.VMEM((288, NLAG), F32),
             pltpu.VMEM((2048, NLAG), BF16),
             pltpu.VMEM((512, 128), F32),
             pltpu.VMEM((64, 4, NLAG), BF16),
@@ -611,7 +659,7 @@
             dma((2,)),
             dma,
             dma,
-            dma((2, 4, 4)),
+            dma((2, 2, 4, 4)),
             dma,
             dma,
         ],

time: 44.3 us -> 44.4 us (level)
  no operation moved by 1% of the time
where the time goes in v4:
time: 44.4 us; the launch traced here: 44.3 us
  Pallas kernels  43.5 us (98%)
  local copies, waits for them, and re-layouts  0.8 us (2%)
    pallas_call x1, Pallas kernels, on_device(): pl.pallas_call(kernel, out_shape=jax.ShapeDtypeStruct((2, 64, 4, NLAG), B...  43.5 us

profile of v4, /device:TPU:1, one launch (start us, length us, event | category | flops | bytes accessed | tf_op | source)
XLA Modules:
  0.0 44.3 jit_solution(1861221556603470455)
XLA Ops:
  0.0 43.5 %shard_map.46 = bf16[2,64,4,512]{3,2,1,0:T(4,128)(2,1)S(1)} custom-call(s32[2]{0:T(128)} %panel_ids_ref.1, bf16[4,4,2048]{2,1,0:T(4,128)(2,1)} %x_hbm.1, s32[4,2048]{1,0:T(4,128)} %bitcast.1, bf16[2944,512]{1,0:T(8,128)(2,1)} %constant.2.clone.tables_hbm), custom_call_target="tpu_custom_call" | custom-call | tf_op jit(solution)/shard_map/pallas_call | solution.py:633
  43.5 0.8 %copy.6 = bf16[2,64,4,512]{3,2,1,0:T(4,128)(2,1)} copy(bf16[2,64,4,512]{3,2,1,0:T(4,128)(2,1)S(1)} %shard_map.46) | data formatting | bytes 1048576
